TPU v7x, 512 devices: a whole 4x8x8 slice. The times are simulated.
512 devices in a mesh: prow: 16 (over x, z_hi), pcol: 32 (over z_lo, y, core).
Axes of the slice: x: 4, y: 8, z: 8 (z_hi: 4, z_lo: 2; z = z_hi * 2 + z_lo), core: 2. Of those that a mesh axis runs over, the one named last changes fastest.
Arguments:
- ancestor_inverse: bfloat16 [24576, 24576], P('pcol', 'prow'), may hold values from -6 to 6
- lower_panel: bfloat16 [24576, 1024], P(('prow', 'pcol')), may hold values from -0.3125 to 0.3125
- pivot_inverse: float32 [256, 1024], P('pcol', 'prow'), may hold values from -6 to 6
- struct_list: int32 [4, 48], replicated, may hold values from -1 to 95, as said below
Outputs:
- off_inverse: bfloat16 [24576, 1024], P('pcol', 'prow')
- diag_inverse: float32 [256, 1024], P('pcol', 'prow')
Inputs may be any that keep to these rules, and one draw needn't show every extreme that they name: `struct_list`: each row lists distinct ancestor supernodes first, all within 48 cyclically consecutive ancestor numbers, then entries -1; every row has at least one ancestor and some row lists 48.
All inputs are finite; a program needn't handle non-finite values.
Results may differ from a plain program's by a relative error of at most 0.001.
Values may be sent and summed in bfloat16 or wider, within the bound.
A program may use at most 64 MiB of HBM per device.

v0:
```python
import jax
import jax.numpy as jnp
from jax import lax
from jax.sharding import PartitionSpec as P

B = 256
NK = 4


def from_root(value, axis, root):
    mine = lax.axis_index(axis) == root
    return lax.psum(jnp.where(mine, value, jnp.zeros_like(value)), axis)


def membership(struct_list, ancestor_ids):
    listed = struct_list[:, :, None] == ancestor_ids[None, None, :]
    return jnp.transpose(jnp.any(listed, axis=1))


def body(ancestor_inverse, lower_panel, pivot_inverse, struct_list):
    row_count = ancestor_inverse.shape[0] // B
    col_count = ancestor_inverse.shape[1] // B
    grid_rows = lax.axis_size("prow")
    prow_index = lax.axis_index("prow")
    pcol_index = lax.axis_index("pcol")
    col_share = NK * B // grid_rows
    gathered = lax.all_gather(lower_panel, "pcol", axis=0, tiled=True)
    col_ids = prow_index * col_count + jnp.arange(col_count, dtype=jnp.int32)
    row_ids = pcol_index * row_count + jnp.arange(row_count, dtype=jnp.int32)
    member_cols = membership(struct_list, col_ids)
    member_rows = membership(struct_list, row_ids)
    scaled = gathered.reshape(col_count, B, NK, B) * member_cols[:, None, :, None].astype(
        jnp.bfloat16
    )
    masked = scaled.reshape(col_count * B, NK * B)
    partial_value = -jnp.dot(ancestor_inverse, masked, preferred_element_type=jnp.float32)
    share_sum = lax.psum_scatter(partial_value, "prow", scatter_dimension=1, tiled=True)
    columns = prow_index * col_share + jnp.arange(col_share, dtype=jnp.int32)
    block_of = columns // B
    one_hot = block_of[:, None] == jnp.arange(NK, dtype=jnp.int32)[None, :]
    row_mask = jnp.any(member_rows[:, None, :] & one_hot[None, :, :], axis=2).astype(jnp.float32)
    off_share = (share_sum.reshape(row_count, B, col_share) * row_mask[:, None, :]).reshape(
        row_count * B, col_share
    )
    off_inverse = off_share.astype(jnp.bfloat16)
    block_count = max(col_share // B, 1)
    column_width = col_share // block_count
    offset_blocks = pcol_index * row_count % col_count
    root_row = pcol_index * row_count // col_count
    piece = lax.dynamic_slice_in_dim(masked, offset_blocks * B, row_count * B, 0)
    lower_rows = from_root(piece, "prow", root_row)
    first_block = prow_index * col_share // B
    lower_slice = lax.dynamic_slice_in_dim(lower_rows, first_block * B, block_count * B, 1)
    lower_blocks = lower_slice.astype(jnp.float32).reshape(row_count * B, block_count, B)
    off_blocks = off_share.reshape(row_count * B, block_count, column_width)
    diag_term = jnp.einsum(
        "ikr,ikc->rkc", lower_blocks, off_blocks, precision=lax.Precision.HIGHEST
    ).reshape(B, col_share)
    diag_share = lax.psum_scatter(diag_term, "pcol", scatter_dimension=0, tiled=True)
    diag_inverse = pivot_inverse - diag_share
    return (off_inverse, diag_inverse)


def solution(mesh):
    placed = (P("pcol", "prow"), P(("prow", "pcol"), None), P("pcol", "prow"), P())
    return jax.shard_map(
        body,
        mesh=mesh,
        in_specs=placed,
        out_specs=(P("pcol", "prow"), P("pcol", "prow")),
        check_vma=False,
    )
```

profile of v0, /device:TPU:25, one launch (start us, length us, event | category | flops | bytes accessed | tf_op | source)
XLA Modules:
  0.0 580.3 jit_solution(7268216275840129706)
XLA Ops:
  7.2 0.0 copy-start
  7.2 0.0 all-gather.2.cloned.1.call-start
  7.2 0.7 all-gather.2.cloned.1.call-update
  7.9 0.0 all-reduce.4.cloned.1.call-start
  8.0 0.9 compare_reduce_fusion
  8.9 0.9 mul.43
  9.8 2.5 copy.20
  12.3 69.3 %all-gather.2.cloned.1.call-done = bf16[1536,1024]{1,0:T(8,128)(2,1)} async-done(((bf16[48,1024]{1,0:T(8,128)(2,1)}), bf16[1536,1024]{1,0:T(8,128)(2,1)}) %all-gather.2.cloned.1.call-update) | async-done | bytes 3145744 | tf_op jit(solution)/shard_map/all_gather | solution.py:27
  81.6 4.4 mul.45
  86.0 0.0 copy-start.1
  86.0 1.7 copy-done.1
  87.7 1.6 dynamic-slice_select_fusion
  89.3 0.0 all-reduce.4.cloned.1.call-update
  89.3 0.0 reduce-scatter.3.cloned.1.call-start
  89.4 6.2 %negate_bitcast_fusion = f32[768,1024]{0,1:T(8,128)} fusion(bf16[1536,1024]{1,0:T(8,128)(2,1)} %copy-done.1, bf16[768,1536]{1,0:T(8,128)(2,1)S(1)} %copy-done), kind=kOutput, calls=%fused_computation | convolution fusion | flops 2416705536 | bytes 8650752 | tf_op jit(solution)/shard_map/dot_general | solution.py:36
  95.6 0.0 reduce-scatter.3.cloned.1.call-update
  95.7 0.0 all-reduce.6.cloned.1.call-start
  95.7 0.6 copy-done.2
  96.3 0.2 compare_reduce_fusion.1
  96.5 0.1 and_reduce_fusion
  96.6 0.1 copy.15
  96.7 0.1 mul.48
  96.9 0.1 copy.16
  97.0 1.3 dynamic-slice
  98.9 161.5 %all-reduce.4.cloned.1.call-done = bf16[768,1024]{1,0:T(8,128)(2,1)} async-done(((bf16[768,1024]{1,0:T(8,128)(2,1)}), bf16[768,1024]{1,0:T(8,128)(2,1)}) %all-reduce.4.cloned.1.call-update) | async-done | bytes 1572880 | tf_op jit(solution)/shard_map/psum | solution.py:12
  260.4 109.3 %reduce-scatter.3.cloned.1.call-done = f32[768,64]{0,1:T(8,128)} async-done(((f32[768,1024]{0,1:T(8,128)}), f32[768,64]{0,1:T(8,128)}) %reduce-scatter.3.cloned.1.call-update) | async-done | bytes 196624 | tf_op jit(solution)/shard_map/reduce_scatter | solution.py:37
  369.7 2.0 convolution_bitcast_fusion
  371.8 0.0 all-reduce.6.cloned.1.call-update
  371.8 1.6 multiply_convert_fusion
  373.4 198.9 %all-reduce.6.cloned.1.call-done = f32[256,64]{0,1:T(8,128)} async-done(((f32[256,64]{0,1:T(8,128)}), f32[256,64]{0,1:T(8,128)}) %all-reduce.6.cloned.1.call-update) | async-done | bytes 65552
  572.3 0.8 dynamic-slice_subtract_fusion
  573.1 0.7 copy.17
  (11 shorter events, 0.1 us)
Async XLA Ops:
  7.2 82.2 %copy-start = (bf16[768,1536]{1,0:T(8,128)(2,1)S(1)}, bf16[768,1536]{1,0:T(8,128)(2,1)}, u32[]{:S(2)}) copy-start(bf16[768,1536]{1,0:T(8,128)(2,1)} %param.4) | copy-start | bytes 7077892
  7.2 74.5 %all-gather.2.cloned.1.call-start = ((), (), s32[]{:S(2)}) async-start(), calls=%async_computation.1 | async-start | bytes 3244032 | tf_op jit(solution)/shard_map/all_gather | solution.py:27
  7.9 252.5 %all-reduce.4.cloned.1.call-start = ((), (), s32[]{:S(2)}) async-start(), calls=%async_computation.3 | async-start | bytes 3145728 | tf_op jit(solution)/shard_map/psum | solution.py:12
  86.0 1.7 copy-start.1
  89.3 280.4 %reduce-scatter.3.cloned.1.call-start = ((), (), s32[]{:S(2)}) async-start(), calls=%async_computation.2 | async-start | bytes 3342336 | tf_op jit(solution)/shard_map/reduce_scatter | solution.py:37
  95.6 0.7 copy-start.2
  95.6 1.3 copy-start.3
  95.7 476.6 %all-reduce.6.cloned.1.call-start = ((), (), s32[]{:S(2)}) async-start(), calls=%async_computation.4 | async-start | bytes 131072
Sparse Core Ops, SparseCore 0:
  10.1 71.4 all-gather.1
  89.4 170.8 all-reduce.3
  264.6 105.0 reduce-scatter.2
  372.5 199.7 all-reduce.5
where the time goes:
time: 581 us; the launch traced here: 580 us
  waiting for transfers between devices  540 us (93%)
  between operations  14.6 us (3%)
  other arithmetic  9.68 us (2%)
  matrix products  8.29 us (1%)
  local copies, waits for them, and re-layouts  7.86 us (1%)
    unnamed x5, waiting for transfers between devices  200 us
    psum x1, waiting for transfers between devices, from_root(): return lax.psum(jnp.where(mine, value, jnp.zeros_like(value)), axis)  161 us
    reduce_scatter x1, waiting for transfers between devices, body(): lax.psum_scatter(partial_value, 'prow', scatter_dimension=1, tiled=True)  109 us
    all_gather x1, waiting for transfers between devices, body(): gathered = lax.all_gather(lower_panel, 'pcol', axis=0, tiled=True)  69.3 us
  transfers between devices with their start and end apart: 4, of which 4 were waited for; matrix products, arithmetic and copies ran while one was open for 2% of the time, Pallas kernels for 0%

commit v1 on v0

--- a/solution.py
+++ b/solution.py
@@ -7,9 +7,15 @@
 NK = 4
 
 
+def add_all(x, axis):
+    parts = lax.all_gather(x, axis, axis=0, tiled=False)
+    summed = parts.sum(axis=0)
+    return summed
+
+
 def from_root(value, axis, root):
     mine = lax.axis_index(axis) == root
-    return lax.psum(jnp.where(mine, value, jnp.zeros_like(value)), axis)
+    return add_all(jnp.where(mine, value, jnp.zeros_like(value)), axis)
 
 
 def membership(struct_list, ancestor_ids):

time: 581 us -> 695 us (1.20)
  waiting for transfers between devices: 540 us -> 638 us
  other arithmetic: 9.68 us -> 24.6 us
    all_gather x0 -> x1, waiting for transfers between devices: none -> 281 us  [add_all(): parts = lax.all_gather(x, axis, axis=0, tiled=False)]
    psum x1 -> x0, waiting for transfers between devices: 161 us -> none  [from_root(): return lax.psum(jnp.where(mine, value, jnp.zeros_like(value)), axis)]
    reduce_scatter x1, waiting for transfers between devices: 109 us -> 88.5 us  [body(): lax.psum_scatter(partial_value, 'prow', scatter_dimension=1, tiled=True)]
    reduce_sum x0 -> x1, other arithmetic: none -> 15 us  [add_all(): summed = parts.sum(axis=0)]
  transfers between devices with their start and end apart: 4 -> 4, of which waited for: 4 -> 4; matrix products, arithmetic and copies ran while one was open for 2% -> 4% of each run, Pallas kernels for 0% -> 0%
where the time goes in v1:
time: 695 us; the launch traced here: 694 us
  waiting for transfers between devices  638 us (92%)
  other arithmetic  24.6 us (4%)
  between operations  14.6 us (2%)
  matrix products  8.35 us (1%)
  local copies, waits for them, and re-layouts  7.94 us (1%)
    all_gather x1, waiting for transfers between devices, add_all(): parts = lax.all_gather(x, axis, axis=0, tiled=False)  281 us
    unnamed x5, waiting for transfers between devices  200 us
    reduce_scatter x1, waiting for transfers between devices, body(): lax.psum_scatter(partial_value, 'prow', scatter_dimension=1, tiled=True)  88.5 us
    all_gather x1, waiting for transfers between devices, body(): gathered = lax.all_gather(lower_panel, 'pcol', axis=0, tiled=True)  69.3 us
    reduce_sum x1, other arithmetic, add_all(): summed = parts.sum(axis=0)  15 us
  transfers between devices with their start and end apart: 4, of which 4 were waited for; matrix products, arithmetic and copies ran while one was open for 4% of the time, Pallas kernels for 0%

profile of v1, /device:TPU:25, one launch (start us, length us, event | category | flops | bytes accessed | tf_op | source)
XLA Modules:
  0.0 694.1 jit_solution(2778156397415640099)
XLA Ops:
  7.2 0.0 copy-start
  7.2 0.0 all-gather.4.cloned.1.call-start
  7.2 0.7 all-gather.4.cloned.1.call-update
  7.9 0.0 all-gather.6.cloned.1.call-start
  8.0 0.9 compare_reduce_fusion
  9.0 0.9 mul.43
  9.8 2.5 copy.20
  12.3 69.3 %all-gather.4.cloned.1.call-done = bf16[1536,1024]{1,0:T(8,128)(2,1)} async-done(((bf16[48,1024]{1,0:T(8,128)(2,1)}), bf16[1536,1024]{1,0:T(8,128)(2,1)}) %all-gather.4.cloned.1.call-update) | async-done | bytes 3145744 | tf_op jit(solution)/shard_map/all_gather | solution.py:33
  81.6 4.4 mul.45
  86.0 1.7 copy-done.1
  87.8 1.6 dynamic-slice_select_fusion
  89.3 0.0 all-gather.6.cloned.1.call-update
  89.3 0.0 reduce-scatter.3.cloned.1.call-start
  89.4 6.3 negate_bitcast_fusion
  95.7 0.0 reduce-scatter.3.cloned.1.call-update
  95.7 0.0 all-reduce.3.cloned.1.call-start
  95.8 0.6 copy-done.2
  96.4 0.2 compare_reduce_fusion.1
  96.6 0.1 and_reduce_fusion
  96.7 0.1 copy.15
  96.8 0.1 copy.16
  96.9 0.1 mul.48
  97.1 1.3 dynamic-slice
  99.0 281.1 %all-gather.6.cloned.1.call-done = bf16[12288,1024]{1,0:T(8,128)(2,1)} async-done(((bf16[768,1024]{1,0:T(8,128)(2,1)}), bf16[12288,1024]{1,0:T(8,128)(2,1)}) %all-gather.6.cloned.1.call-update) | async-done | bytes 25165840 | tf_op jit(solution)/shard_map/all_gather | solution.py:11
  380.1 15.0 %reduce_sum.12 = bf16[768,1024]{1,0:T(8,128)(2,1)} reduce(bf16[16,768,1024]{2,1,0:T(8,128)(2,1)} %bitcast.24, bf16[]{:T(256)} %constant.61.clone.1), dimensions={0}, to_apply=%region_4.5 | reduce | flops 11796480 | bytes 26738690 | tf_op jit(solution)/shard_map/reduce_sum | solution.py:12
  395.1 88.5 %reduce-scatter.3.cloned.1.call-done = f32[768,64]{0,1:T(8,128)} async-done(((f32[768,1024]{0,1:T(8,128)}), f32[768,64]{0,1:T(8,128)}) %reduce-scatter.3.cloned.1.call-update) | async-done | bytes 196624 | tf_op jit(solution)/shard_map/reduce_scatter | solution.py:43
  483.6 2.0 convolution_bitcast_fusion
  485.6 0.0 all-reduce.3.cloned.1.call-update
  485.6 1.6 multiply_convert_fusion
  487.2 198.9 %all-reduce.3.cloned.1.call-done = f32[256,64]{0,1:T(8,128)} async-done(((f32[256,64]{0,1:T(8,128)}), f32[256,64]{0,1:T(8,128)}) %all-reduce.3.cloned.1.call-update) | async-done | bytes 65552
  686.1 0.8 dynamic-slice_subtract_fusion
  686.9 0.7 copy.17
  (12 shorter events, 0.1 us)
Async XLA Ops:
  7.2 82.2 %copy-start = (bf16[768,1536]{1,0:T(8,128)(2,1)S(1)}, bf16[768,1536]{1,0:T(8,128)(2,1)}, u32[]{:S(2)}) copy-start(bf16[768,1536]{1,0:T(8,128)(2,1)} %param.4) | copy-start | bytes 7077892
  7.2 74.5 %all-gather.4.cloned.1.call-start = ((), (), s32[]{:S(2)}) async-start(), calls=%async_computation.1 | async-start | bytes 3244032 | tf_op jit(solution)/shard_map/all_gather | solution.py:33
  7.9 372.2 %all-gather.6.cloned.1.call-start = ((), (), s32[]{:S(2)}) async-start(), calls=%async_computation.3 | async-start | bytes 26738688 | tf_op jit(solution)/shard_map/all_gather | solution.py:11
  86.0 1.8 copy-start.1
  89.3 394.2 %reduce-scatter.3.cloned.1.call-start = ((), (), s32[]{:S(2)}) async-start(), calls=%async_computation.2 | async-start | bytes 3342336 | tf_op jit(solution)/shard_map/reduce_scatter | solution.py:43
  95.7 0.7 copy-start.2
  95.7 1.1 copy-start.3
  95.7 590.3 %all-reduce.3.cloned.1.call-start = ((), (), s32[]{:S(2)}) async-start(), calls=%async_computation.4 | async-start | bytes 131072
Sparse Core Ops, SparseCore 0:
  10.1 71.4 all-gather.3
  89.5 290.6 all-gather.5
  384.3 99.1 reduce-scatter.2
  486.3 199.7 all-reduce.2
